TPU v7x, 128 devices: a whole 4x4x4 slice. The times are simulated.
128 devices in a mesh: seq: 4 (over z_lo, core), res: 32 (over y, x, z_hi).
Axes of the slice: x: 4, y: 4, z: 4 (z_hi: 2, z_lo: 2; z = z_hi * 2 + z_lo), core: 2. Of those that a mesh axis runs over, the one named last changes fastest.
Arguments:
- homolog_embedding: bfloat16 [16, 2048, 256], P('seq', 'res'), may hold values from -6 to 6
- pair_input_rows: bfloat16 [2048, 2048, 128], P('res', 'seq'), may hold values from -256 to 256
- incoming_slope: bfloat16 [16, 2048, 256], P('seq', 'res'), may hold values from -6 to 6
- rescale_factor: float32 [256], replicated, may hold values from 0.25 to 1.75
- probe_weights: bfloat16 [256, 256], replicated, may hold values from -0.375 to 0.375
- lookup_weights: bfloat16 [256, 256], replicated, may hold values from -0.375 to 0.375
- content_weights: bfloat16 [256, 256], replicated, may hold values from -0.375 to 0.375
- sigmoid_weights: bfloat16 [256, 256], replicated, may hold values from -0.375 to 0.375
- final_projection: bfloat16 [256, 256], replicated, may hold values from -0.375 to 0.375
- pair_bias_matrix: bfloat16 [128, 8], replicated, may hold values from -1 to 1
Outputs:
- alignment_rows_gradient: bfloat16 [16, 2048, 256], P('seq', 'res')
- pair_input_gradient: bfloat16 [2048, 2048, 128], P('res', 'seq')
- layer_gain_gradient: float32 [256], replicated
- query_matrix_gradient: float32 [256, 256], replicated
- key_matrix_gradient: float32 [256, 256], replicated
- value_matrix_gradient: float32 [256, 256], replicated
- gate_matrix_gradient: float32 [256, 256], replicated
- final_projection_slope: float32 [256, 256], replicated
- pair_bias_matrix_gradient: float32 [128, 8], replicated
All inputs are finite; a program needn't handle non-finite values.
Results may differ from a plain program's by a relative error of at most 0.0034.
The roundings to bfloat16 on the way count: a program that leaves them out, or rounds other values in their place, can miss the bound.
Values may be sent and summed in bfloat16 or wider, within the bound.
A program may use at most 128 MiB of HBM per device.

v0:
```python
import functools
import math
import jax
import jax.numpy as jnp
from jax import lax
from jax.sharding import PartitionSpec as P


def layer_norm_rows(alignment_block):
    content_vectors = alignment_block.astype(jnp.float32)
    centered = content_vectors - jnp.mean(content_vectors, axis=-1, keepdims=True)
    inverse_deviation = lax.rsqrt(jnp.mean(centered * centered, axis=-1, keepdims=True) + 1e-05)
    return (centered * inverse_deviation, inverse_deviation)


def row_backward(bias_full, head_count, dbias_total, row_inputs):
    probe_vectors, keys_row, values_row, gate_row, derivative_modulated = row_inputs
    query_total, channel_width = probe_vectors.shape
    key_count = keys_row.shape[0]
    head_width = channel_width // head_count
    softmax_scale = 1.0 / math.sqrt(head_width)
    query_heads = probe_vectors.reshape(query_total, head_count, head_width)
    key_heads = keys_row.reshape(key_count, head_count, head_width)
    value_heads = values_row.reshape(key_count, head_count, head_width)
    scores = (
        jnp.einsum("ihd,jhd->hij", query_heads, key_heads, preferred_element_type=jnp.float32)
        * softmax_scale
    )
    scores = scores + bias_full.astype(jnp.float32)
    weights_soft = jax.nn.softmax(scores, axis=-1)
    weights_half = weights_soft.astype(jnp.bfloat16)
    attended = jnp.einsum(
        "hij,jhd->ihd", weights_half, value_heads, preferred_element_type=jnp.float32
    ).reshape(query_total, channel_width)
    modulated_result = (gate_row * attended).astype(jnp.bfloat16)
    grad_attended = (derivative_modulated * gate_row).astype(jnp.bfloat16)
    derivative_logits_sigmoid = (
        derivative_modulated * attended * gate_row * (1.0 - gate_row)
    ).astype(jnp.bfloat16)
    grad_heads = grad_attended.reshape(query_total, head_count, head_width)
    grad_weights = jnp.einsum(
        "ihd,jhd->hij", grad_heads, value_heads, preferred_element_type=jnp.float32
    )
    row_inner = jnp.sum(weights_soft * grad_weights, axis=-1, keepdims=True)
    grad_scores = weights_soft * (grad_weights - row_inner)
    scores_half = grad_scores.astype(jnp.bfloat16)
    derivative_probe_weights = (
        jnp.einsum("hij,jhd->ihd", scores_half, key_heads, preferred_element_type=jnp.float32)
        * softmax_scale
    ).astype(jnp.bfloat16)
    derivative_lookup_weights = (
        jnp.einsum("hij,ihd->jhd", scores_half, query_heads, preferred_element_type=jnp.float32)
        * softmax_scale
    )
    derivative_content_weights = jnp.einsum(
        "hij,ihd->jhd", weights_half, grad_heads, preferred_element_type=jnp.float32
    )
    outputs = (
        modulated_result,
        derivative_logits_sigmoid,
        derivative_probe_weights.reshape(query_total, channel_width),
        derivative_lookup_weights.reshape(key_count, channel_width),
        derivative_content_weights.reshape(key_count, channel_width),
    )
    return (dbias_total + grad_scores, outputs)


def body(
    homolog_embedding,
    pair_input_rows,
    incoming_slope,
    rescale_factor,
    probe_weights,
    lookup_weights,
    content_weights,
    sigmoid_weights,
    final_projection,
    pair_bias_matrix,
):
    highest = lax.Precision.HIGHEST
    head_count = pair_bias_matrix.shape[1]
    row_total, query_total, channel_width = homolog_embedding.shape
    standardized_rows, inverse_deviation = layer_norm_rows(homolog_embedding)
    rescaled_embedding = (standardized_rows * rescale_factor).astype(jnp.bfloat16)
    rescaled_plain = rescaled_embedding.reshape(-1, channel_width)
    probe_vectors = (
        jnp.dot(rescaled_plain, probe_weights, preferred_element_type=jnp.float32)
        .astype(jnp.bfloat16)
        .reshape(row_total, query_total, channel_width)
    )
    sigmoid_factors = jax.nn.sigmoid(
        jnp.dot(rescaled_plain, sigmoid_weights, preferred_element_type=jnp.float32)
    ).reshape(row_total, query_total, channel_width)
    incoming_slope_plain = incoming_slope.reshape(-1, channel_width)
    derivative_modulated = jnp.dot(
        incoming_slope_plain, final_projection.T, preferred_element_type=jnp.float32
    ).reshape(row_total, query_total, channel_width)
    bias_local = jnp.einsum(
        "ijc,ch->hij", pair_input_rows, pair_bias_matrix, preferred_element_type=jnp.float32
    ).astype(jnp.bfloat16)
    bias_full = lax.all_gather(bias_local, "seq", axis=2, tiled=True)
    normed_all = lax.all_gather(rescaled_embedding, "res", axis=1, tiled=True)
    key_count = normed_all.shape[1]
    all_flat = normed_all.reshape(-1, channel_width)
    lookup_vectors = (
        jnp.dot(all_flat, lookup_weights, preferred_element_type=jnp.float32)
        .astype(jnp.bfloat16)
        .reshape(row_total, key_count, channel_width)
    )
    content_vectors = (
        jnp.dot(all_flat, content_weights, preferred_element_type=jnp.float32)
        .astype(jnp.bfloat16)
        .reshape(row_total, key_count, channel_width)
    )
    dbias_init = jnp.zeros(bias_full.shape, jnp.float32)
    dbias_local, row_results = lax.scan(
        functools.partial(row_backward, bias_full, head_count),
        dbias_init,
        (probe_vectors, lookup_vectors, content_vectors, sigmoid_factors, derivative_modulated),
    )
    (
        modulated_result,
        derivative_logits_sigmoid,
        derivative_probe_weights,
        derivative_lookup_weights,
        derivative_content_weights,
    ) = row_results
    key_weight_wide = lookup_weights.astype(jnp.float32)
    value_weight_wide = content_weights.astype(jnp.float32)
    lookup_plain = derivative_lookup_weights.reshape(-1, channel_width)
    content_plain = derivative_content_weights.reshape(-1, channel_width)
    key_term = (
        jnp.dot(lookup_plain, key_weight_wide.T, precision=highest)
        + jnp.dot(content_plain, value_weight_wide.T, precision=highest)
    ).reshape(row_total, -1, channel_width)
    grad_from_keys = lax.psum_scatter(key_term, "res", scatter_dimension=1, tiled=True).reshape(
        -1, channel_width
    )
    all_wide = all_flat.astype(jnp.float32)
    part_key = jnp.dot(all_wide.T, lookup_plain, precision=highest)
    part_value = jnp.dot(all_wide.T, content_plain, precision=highest)
    probe_plain = derivative_probe_weights.reshape(-1, channel_width)
    sigmoid_factor_plain = derivative_logits_sigmoid.reshape(-1, channel_width)
    part_query = jnp.dot(rescaled_plain.T, probe_plain, preferred_element_type=jnp.float32)
    part_gate = jnp.dot(rescaled_plain.T, sigmoid_factor_plain, preferred_element_type=jnp.float32)
    part_out = jnp.dot(
        modulated_result.reshape(-1, channel_width).T,
        incoming_slope_plain,
        preferred_element_type=jnp.float32,
    )
    derivative_rescaled = (
        jnp.dot(probe_plain, probe_weights.T, preferred_element_type=jnp.float32)
        + jnp.dot(sigmoid_factor_plain, sigmoid_weights.T, preferred_element_type=jnp.float32)
        + grad_from_keys
    )
    derivative_rescaled = derivative_rescaled.reshape(row_total, query_total, channel_width)
    part_gain = jnp.sum(derivative_rescaled * standardized_rows, axis=(0, 1))
    centered_scaled_gradient = derivative_rescaled * rescale_factor
    alignment_rows_gradient = (
        inverse_deviation
        * (
            centered_scaled_gradient
            - jnp.mean(centered_scaled_gradient, axis=-1, keepdims=True)
            - standardized_rows
            * jnp.mean(centered_scaled_gradient * standardized_rows, axis=-1, keepdims=True)
        )
    ).astype(jnp.bfloat16)
    dbias_own = lax.psum_scatter(dbias_local, "seq", scatter_dimension=2, tiled=True).astype(
        jnp.bfloat16
    )
    pair_input_gradient = jnp.einsum(
        "hij,ch->ijc", dbias_own, pair_bias_matrix, preferred_element_type=jnp.float32
    ).astype(jnp.bfloat16)
    part_bias = jnp.einsum(
        "ijc,hij->ch", pair_input_rows, dbias_own, preferred_element_type=jnp.float32
    )
    totals = lax.psum(
        (part_gain, part_query, part_key, part_value, part_gate, part_out, part_bias),
        ("seq", "res"),
    )
    return (
        alignment_rows_gradient,
        pair_input_gradient,
        totals[0],
        totals[1],
        totals[2],
        totals[3],
        totals[4],
        totals[5],
        totals[6],
    )


def solution(mesh):
    in_specs = (
        P("seq", "res", None),
        P("res", "seq", None),
        P("seq", "res", None),
        P(),
        P(),
        P(),
        P(),
        P(),
        P(),
        P(),
    )
    out_specs = (P("seq", "res", None), P("res", "seq", None), P(), P(), P(), P(), P(), P(), P())
    return jax.shard_map(body, mesh=mesh, in_specs=in_specs, out_specs=out_specs, check_vma=False)
```

profile of v0, /device:TPU:1, one launch (start us, length us, event | category | flops | bytes accessed | tf_op | source)
XLA Modules:
  0.0 668.8 jit_solution(14989727427753423162)
XLA Ops:
  7.3 6.7 convolution_convert_fusion.3
  18.7 28.2 %all-gather.5.cloned.1.call-done = bf16[8,64,2048]{2,0,1:T(8,128)(2,1)} async-done(((bf16[8,64,512]{2,0,1:T(8,128)(2,1)}), bf16[8,64,2048]{2,0,1:T(8,128)(2,1)}) %all-gather.5.cloned.1.call-update) | async-done | bytes 2097168 | tf_op jit(solution)/shard_map/all_gather | solution.py:101
  46.9 4.1 copy.34
  51.0 80.8 %all-gather.3.cloned.1.call-done = bf16[4,2048,256]{2,1,0:T(8,128)(2,1)} async-done(((bf16[4,64,256]{2,1,0:T(8,128)(2,1)}), bf16[4,2048,256]{2,1,0:T(8,128)(2,1)}) %all-gather.3.cloned.1.call-update) | async-done | bytes 4194320 | tf_op jit(solution)/shard_map/all_gather | solution.py:102
  131.8 5.6 convolution_convert_fusion
  137.4 3.2 convolution_convert_fusion.1
  140.6 105.2 %while.21 = (s32[]{:T(128)}, f32[8,64,2048]{2,1,0:T(8,128)}, bf16[4,64,256]{1,2,0:T(8,128)(2,1)}, bf16[4,64,256]{1,2,0:T(8,128)(2,1)}, bf16[4,64,256]{1,2,0:T(8,...) while((s32[]{:T(128)}, f32[8,64,2048]{2,1,0:T(8,128)}, ...), condition=%wide.region_6.7_spmd.clone, body=%wide.region_2.6_spmd.clone.sunk | while | flops 422233600 | bytes 126007688 | solution.py:116
  145.4 4.9 fusion.108
  150.3 3.1 fusion.109
  158.8 3.5 fusion.111
  171.7 4.9 fusion.108
  176.6 3.1 fusion.109
  185.1 3.5 fusion.111
  198.0 4.9 fusion.108
  202.9 3.1 fusion.109
  208.1 2.8 multiply_reduce_fusion.3
  211.4 3.5 fusion.111
  224.3 4.9 fusion.108
  229.2 3.1 fusion.109
  234.4 2.8 multiply_reduce_fusion.3
  237.6 3.5 fusion.111
  246.1 8.8 %copy.40 = f32[4,2048,256]{2,1,0:T(8,128)} copy(f32[4,2048,256]{1,2,0:T(8,128)} %get-tuple-element.83) | data formatting | bytes 16777216 | tf_op jit(solution)/shard_map/while | solution.py:116
  254.8 8.7 %copy.41 = f32[4,2048,256]{2,1,0:T(8,128)} copy(f32[4,2048,256]{1,2,0:T(8,128)} %get-tuple-element.84) | data formatting | bytes 16777216 | tf_op jit(solution)/shard_map/while | solution.py:116
  263.6 6.7 %fusion.38 = f32[8192,256]{1,0:T(8,128)S(1)} fusion(f32[8192,256]{1,0:T(8,128)} %bitcast.143, bf16[256,256]{1,0:T(8,128)(2,1)S(1)} %copy-done), kind=kOutput, calls=%fused_computation.79 | convolution fusion | flops 6442450944 | bytes 16908288 | tf_op jit(solution)/shard_map/dot_general | solution.py:133
  270.3 6.4 convolution_add_fusion
  281.1 11.1 %convolution_bitcast_fusion.2 = f32[256,256]{1,0:T(8,128)} fusion(bf16[4,2048,256]{2,1,0:T(8,128)(2,1)} %all-gather.3.cloned.1.call-done, f32[4,2048,256]{1,2,0:T(8,128)} %get-tuple-element.84), kind=kOutput, calls=%fused_computation.40 | convolution fusion | flops 6442450944 | bytes 12845056 | tf_op jit(solution)/shard_map/dot_general | solution.py:141
  292.2 8.4 %convolution_bitcast_fusion.3 = f32[256,256]{1,0:T(8,128)} fusion(bf16[4,2048,256]{2,1,0:T(8,128)(2,1)S(1)} %copy-done.5, f32[4,2048,256]{1,2,0:T(8,128)} %get-tuple-element.83), kind=kOutput, calls=%fused_computation.41 | convolution fusion | flops 6442450944 | bytes 12845056 | tf_op jit(solution)/shard_map/dot_general | solution.py:140
  301.9 4.8 convolution_bitcast_fusion.5
  306.8 5.5 convolution_convert_fusion.2
  312.4 165.3 %reduce-scatter.3.cloned.1.call-done = f32[4,64,256]{2,1,0:T(8,128)} async-done(((f32[4,2048,256]{2,1,0:T(8,128)}), f32[4,64,256]{2,1,0:T(8,128)}) %reduce-scatter.3.cloned.1.call-update) | async-done | bytes 262160 | tf_op jit(solution)/shard_map/reduce_scatter | solution.py:136
  479.2 84.4 %all-reduce = (f32[256]{0:T(256)}, f32[128,8]{0,1:T(8,128)}) all-reduce(f32[256]{0:T(256)S(1)} %get-tuple-element.155, f32[128,8]{0,1:T(8,128)S(1)} %convolution_bitcast_fusion.5), channel_id=1, replica_groups=mesh['seq'=4,'res'=32] {'seq','res'}, use_global_device_ids=true, to_apply=%region_12.13 | all-reduce | flops 1280 | bytes 10240 | tf_op jit(solution)/shard_map/psum | solution.py:177
  564.5 89.4 %all-reduce.4.cloned.1.call-done = (f32[256,256]{1,0:T(8,128)}, f32[256,256]{1,0:T(8,128)}, f32[256,256]{1,0:T(8,128)}, f32[256,256]{1,0:T(8,128)}, f32[256,256]{1,0:T(8,128)}) async-done(((f32[256,256]{1,0:T(8,128)}, f32[256,256]{1,0:T(8,128)}, f32[256,256]{1,0:T(8,128)}, f32[256,256]{1,0:T(8,128)}, f32[256,256]{1,0:T(8,128)}), (f32[256,256]{1,0:T(8,128)}, f32[256,256]{1,0:T(8,128)}, f32[256,256]{1,0:T(8,128)}, ...) | async-done | bytes 1310736 | tf_op jit(solution)/shard_map/psum | solution.py:177
  (213 shorter events, 74.3 us)
Async XLA Ops:
  7.2 130.2 %copy-start = (bf16[256,256]{1,0:T(8,128)(2,1)S(1)}, bf16[256,256]{1,0:T(8,128)(2,1)}, u32[]{:S(2)}) copy-start(bf16[256,256]{1,0:T(8,128)(2,1)} %param.17) | copy-start | bytes 393220
  7.2 6.9 %copy-start.8 = (bf16[4,64,256]{2,1,0:T(8,128)(2,1)S(1)}, bf16[4,64,256]{2,1,0:T(8,128)(2,1)}, u32[]{:S(2)}) copy-start(bf16[4,64,256]{2,1,0:T(8,128)(2,1)} %param.12) | copy-start | bytes 393220
  7.2 7.2 %copy-start.30 = (f32[256]{0:T(256)S(1)}, f32[256]{0:T(256)}, u32[]{:S(2)}) copy-start(f32[256]{0:T(256)} %param.15) | copy-start | bytes 3076
  7.2 8.2 %copy-start.18 = (bf16[256,256]{1,0:T(8,128)(2,1)S(1)}, bf16[256,256]{1,0:T(8,128)(2,1)}, u32[]{:S(2)}) copy-start(bf16[256,256]{1,0:T(8,128)(2,1)} %param.16) | copy-start | bytes 393220
  7.2 9.3 %copy-start.24 = (bf16[256,256]{1,0:T(8,128)(2,1)S(1)}, bf16[256,256]{1,0:T(8,128)(2,1)}, u32[]{:S(2)}) copy-start(bf16[256,256]{1,0:T(8,128)(2,1)} %param.19) | copy-start | bytes 393220
  7.2 10.4 %copy-start.16 = (bf16[4,64,256]{2,1,0:T(8,128)(2,1)S(1)}, bf16[4,64,256]{2,1,0:T(8,128)(2,1)}, u32[]{:S(2)}) copy-start(bf16[4,64,256]{2,1,0:T(8,128)(2,1)} %param.14) | copy-start | bytes 393220
  7.3 10.4 %copy-start.23 = (bf16[256,256]{1,0:T(8,128)(2,1)S(1)}, bf16[256,256]{1,0:T(8,128)(2,1)}, u32[]{:S(2)}) copy-start(bf16[256,256]{1,0:T(8,128)(2,1)} %param.20) | copy-start | bytes 393220
  7.3 39.7 %all-gather.5.cloned.1.call-start = ((), (), s32[]{:S(2)}) async-start(), calls=%async_computation.3 | async-start | bytes 2621440 | tf_op jit(solution)/shard_map/all_gather | solution.py:101
  14.0 117.8 %copy-start.14 = (bf16[256,256]{1,0:T(8,128)(2,1)S(1)}, bf16[256,256]{1,0:T(8,128)(2,1)}, u32[]{:S(2)}) copy-start(bf16[256,256]{1,0:T(8,128)(2,1)} %param.18) | copy-start | bytes 393220
  14.0 117.8 %all-gather.3.cloned.1.call-start = ((), (), s32[]{:S(2)}) async-start(), calls=%async_computation.2 | async-start | bytes 4325376 | tf_op jit(solution)/shard_map/all_gather | solution.py:102
  15.3 285.4 %reduce-scatter.5.cloned.1.call-start = ((), (), s32[]{:S(2)}) async-start(), calls=%async_computation.5 | async-start | bytes 5242880 | tf_op jit(solution)/shard_map/reduce_scatter | solution.py:168
  131.8 5.6 copy-start.4
  150.3 4.7 copy-start.1
  162.3 4.6 copy-start.3
  176.6 4.7 copy-start.1
  188.6 4.6 copy-start.3
  202.9 4.7 copy-start.1
  214.9 4.6 copy-start.3
  229.2 4.7 copy-start.1
  241.2 4.6 copy-start.3
  245.8 231.8 %reduce-scatter.3.cloned.1.call-start = ((), (), s32[]{:S(2)}) async-start(), calls=%async_computation.4 | async-start | bytes 8650752 | tf_op jit(solution)/shard_map/reduce_scatter | solution.py:136
  263.6 6.7 %copy-start.6 = (f32[4,2048,256]{2,1,0:T(8,128)S(1)}, f32[4,2048,256]{2,1,0:T(8,128)}, u32[]{:S(2)}) copy-start(f32[4,2048,256]{2,1,0:T(8,128)} %copy.41) | copy-start | bytes 25165828
  263.6 6.7 %copy-start.15 = (bf16[256,256]{1,0:T(8,128)(2,1)S(1)}, bf16[256,256]{1,0:T(8,128)(2,1)}, u32[]{:S(2)}) copy-start(bf16[256,256]{1,0:T(8,128)(2,1)} %param.18) | copy-start | bytes 393220
  276.7 4.1 copy-start.19
  276.8 377.2 %all-reduce.4.cloned.1.call-start = ((), (), s32[]{:S(2)}) async-start(), calls=%async_computation.6 | async-start | bytes 2621440 | tf_op jit(solution)/shard_map/psum | solution.py:177
  281.1 11.1 %copy-start.5 = (bf16[4,2048,256]{2,1,0:T(8,128)(2,1)S(1)}, bf16[4,2048,256]{2,1,0:T(8,128)(2,1)}, u32[]{:S(2)}) copy-start(bf16[4,2048,256]{2,1,0:T(8,128)(2,1)} %all-gather.3.cloned.1.call-done) | copy-start | bytes 12582916
  301.9 4.8 copy-start.32
  306.8 170.9 %copy-start.25 = (bf16[256,256]{1,0:T(8,128)(2,1)S(1)}, bf16[256,256]{1,0:T(8,128)(2,1)}, u32[]{:S(2)}) copy-start(bf16[256,256]{1,0:T(8,128)(2,1)} %param.19) | copy-start | bytes 393220
  306.8 170.9 %copy-start.31 = (f32[256]{0:T(256)S(1)}, f32[256]{0:T(256)}, u32[]{:S(2)}) copy-start(f32[256]{0:T(256)} %param.15) | copy-start | bytes 3076
  306.8 172.2 %copy-start.9 = (bf16[4,64,256]{2,1,0:T(8,128)(2,1)S(1)}, bf16[4,64,256]{2,1,0:T(8,128)(2,1)}, u32[]{:S(2)}) copy-start(bf16[4,64,256]{2,1,0:T(8,128)(2,1)} %param.12) | copy-start | bytes 393220
  306.8 172.2 %copy-start.27 = (f32[4,64]{1,0:T(4,128)S(1)}, f32[4,64]{1,0:T(4,128)}, u32[]{:S(2)}) copy-start(f32[4,64]{1,0:T(4,128)} %copy-done.26) | copy-start | bytes 3076
  306.8 172.2 %copy-start.29 = (f32[4,64]{1,0:T(4,128)S(1)}, f32[4,64]{1,0:T(4,128)}, u32[]{:S(2)}) copy-start(f32[4,64]{1,0:T(4,128)} %copy-done.28) | copy-start | bytes 3076
  (27 other events, 48.8 us)
Sparse Core Ops, SparseCore 0:
  14.1 32.7 all-gather.4
  50.6 81.1 all-gather.2
  246.0 44.0 reduce-scatter.4
  292.3 185.3 reduce-scatter.2
  483.8 170.0 all-reduce.3
where the time goes:
time: 670 us; the launch traced here: 669 us
  waiting for transfers between devices  364 us (54%)
  matrix products  116 us (17%)
  blocking collectives  84.4 us (13%)
  local copies, waits for them, and re-layouts  68.2 us (10%)
  other arithmetic  21.5 us (3%)
  between operations  14.2 us (2%)
    reduce_scatter x1, waiting for transfers between devices, body(): lax.psum_scatter(key_term, 'res', scatter_dimension=1, tiled=True)  165 us
    psum x1, waiting for transfers between devices, body(): lax.psum((part_gain, part_query, part_key, part_value, part_gate, part_ou...  89.4 us
    psum x1, blocking collectives, body(): lax.psum((part_gain, part_query, part_key, part_value, part_gate, part_ou...  84.4 us
    all_gather x1, waiting for transfers between devices, body(): normed_all = lax.all_gather(rescaled_embedding, 'res', axis=1, tiled=True)  80.8 us
    all_gather x1, waiting for transfers between devices, body(): bias_full = lax.all_gather(bias_local, 'seq', axis=2, tiled=True)  28.2 us
    sub x4, matrix products, row_backward(): weights_soft = jax.nn.softmax(scores, axis=-1)  19.8 us
    while x4, local copies, waits for them, and re-layouts, body(): lax.scan(functools.partial(row_backward, bias_full, head_count), dbias_in...  17.7 us
    dynamic_slice x32, local copies, waits for them, and re-layouts, body(): lax.scan(functools.partial(row_backward, bias_full, head_count), dbias_in...  16.4 us
  transfers between devices with their start and end apart: 5, of which 4 were waited for; matrix products, arithmetic and copies ran while one was open for 11% of the time, Pallas kernels for 0%

commit v1 on v0

--- a/solution.py
+++ b/solution.py
@@ -4,6 +4,7 @@
 import jax.numpy as jnp
 from jax import lax
 from jax.sharding import PartitionSpec as P
+from jax.lax import psum
 
 
 def layer_norm_rows(alignment_block):
@@ -174,10 +175,10 @@
     part_bias = jnp.einsum(
         "ijc,hij->ch", pair_input_rows, dbias_own, preferred_element_type=jnp.float32
     )
-    totals = lax.psum(
-        (part_gain, part_query, part_key, part_value, part_gate, part_out, part_bias),
-        ("seq", "res"),
-    )
+    prior = psum(
+        (part_gain, part_query, part_key, part_value, part_gate, part_out, part_bias), "res"
+    )
+    totals = psum(prior, "seq")
     return (
         alignment_rows_gradient,
         pair_input_gradient,

time: 670 us -> 1000 us (1.49)
  waiting for transfers between devices: 364 us -> 657 us
  blocking collectives: 84.4 us -> 121 us
    psum x1 -> x2, waiting for transfers between devices: 89.4 us -> 299 us  [the longest x1 299 us: body(): psum((part_gain, part_query, part_key, part_value, part_gate, part_out, p...]
    reduce_scatter x1, waiting for transfers between devices: 0.02 us -> 71.2 us  [body(): lax.psum_scatter(dbias_local, 'seq', scatter_dimension=2, tiled=True)]
    psum x1 -> x2, blocking collectives: 84.4 us -> 121 us  [the longest x1 79.5 us: body(): psum((part_gain, part_query, part_key, part_value, part_gate, part_out, p...]
    reduce_scatter x1, waiting for transfers between devices: 165 us -> 177 us  [body(): lax.psum_scatter(key_term, 'res', scatter_dimension=1, tiled=True)]
  transfers between devices with their start and end apart: 5 -> 6, of which waited for: 4 -> 5; matrix products, arithmetic and copies ran while one was open for 11% -> 5% of each run, Pallas kernels for 0% -> 0%
where the time goes in v1:
time: 1000 us; the launch traced here: 999 us
  waiting for transfers between devices  657 us (66%)
  blocking collectives  121 us (12%)
  matrix products  116 us (12%)
  local copies, waits for them, and re-layouts  68.3 us (7%)
  other arithmetic  21.5 us (2%)
  between operations  14.5 us (1%)
    psum x1, waiting for transfers between devices, body(): psum((part_gain, part_query, part_key, part_value, part_gate, part_out, p...  299 us
    reduce_scatter x1, waiting for transfers between devices, body(): lax.psum_scatter(key_term, 'res', scatter_dimension=1, tiled=True)  177 us
    all_gather x1, waiting for transfers between devices, body(): normed_all = lax.all_gather(rescaled_embedding, 'res', axis=1, tiled=True)  80.8 us
    psum x1, blocking collectives, body(): psum((part_gain, part_query, part_key, part_value, part_gate, part_out, p...  79.5 us
    reduce_scatter x1, waiting for transfers between devices, body(): lax.psum_scatter(dbias_local, 'seq', scatter_dimension=2, tiled=True)  71.2 us
    psum x1, blocking collectives, body(): totals = psum(prior, 'seq')  41.3 us
    all_gather x1, waiting for transfers between devices, body(): bias_full = lax.all_gather(bias_local, 'seq', axis=2, tiled=True)  28.2 us
  transfers between devices with their start and end apart: 6, of which 5 were waited for; matrix products, arithmetic and copies ran while one was open for 5% of the time, Pallas kernels for 0%

profile of v1, /device:TPU:1, one launch (start us, length us, event | category | flops | bytes accessed | tf_op | source)
XLA Modules:
  0.0 999.2 jit_solution(7296195740414935652)
XLA Ops:
  7.3 6.7 convolution_convert_fusion.3
  18.7 28.2 %all-gather.5.cloned.1.call-done = bf16[8,64,2048]{2,0,1:T(8,128)(2,1)} async-done(((bf16[8,64,512]{2,0,1:T(8,128)(2,1)}), bf16[8,64,2048]{2,0,1:T(8,128)(2,1)}) %all-gather.5.cloned.1.call-update) | async-done | bytes 2097168 | tf_op jit(solution)/shard_map/all_gather | solution.py:102
  46.9 4.1 copy.34
  51.0 80.8 %all-gather.3.cloned.1.call-done = bf16[4,2048,256]{2,1,0:T(8,128)(2,1)} async-done(((bf16[4,64,256]{2,1,0:T(8,128)(2,1)}), bf16[4,2048,256]{2,1,0:T(8,128)(2,1)}) %all-gather.3.cloned.1.call-update) | async-done | bytes 4194320 | tf_op jit(solution)/shard_map/all_gather | solution.py:103
  131.8 5.5 convolution_convert_fusion
  137.3 3.2 convolution_convert_fusion.1
  140.5 105.6 %while.21 = (s32[]{:T(128)}, f32[8,64,2048]{2,1,0:T(8,128)}, bf16[4,64,256]{1,2,0:T(8,128)(2,1)}, bf16[4,64,256]{1,2,0:T(8,128)(2,1)}, bf16[4,64,256]{1,2,0:T(8,...) while((s32[]{:T(128)}, f32[8,64,2048]{2,1,0:T(8,128)}, ...), condition=%wide.region_6.7_spmd.clone, body=%wide.region_2.6_spmd.clone.sunk | while | flops 422233600 | bytes 126007688 | solution.py:117
  145.3 5.0 fusion.108
  150.2 3.1 fusion.109
  158.7 3.5 fusion.111
  171.6 5.0 fusion.108
  176.6 3.1 fusion.109
  185.1 3.5 fusion.111
  198.0 5.0 fusion.108
  203.0 3.1 fusion.109
  211.4 3.5 fusion.111
  224.3 5.0 fusion.108
  229.3 3.1 fusion.109
  237.8 3.5 fusion.111
  252.0 10.9 %convolution_bitcast_fusion.2 = f32[256,256]{1,0:T(8,128)} fusion(bf16[4,2048,256]{2,1,0:T(8,128)(2,1)} %all-gather.3.cloned.1.call-done, f32[4,2048,256]{1,2,0:T(8,128)} %get-tuple-element.84), kind=kOutput, calls=%fused_computation.40 | convolution fusion | flops 6442450944 | bytes 12845056 | tf_op jit(solution)/shard_map/dot_general | solution.py:142
  262.9 6.1 convolution_bitcast_fusion.3
  269.7 9.0 copy.40
  278.7 8.7 copy.41
  287.3 6.6 fusion.38
  294.0 6.4 convolution_add_fusion
  301.9 298.5 %all-reduce.7.cloned.1.call-done = (f32[256,256]{1,0:T(8,128)}, f32[256,256]{1,0:T(8,128)}, f32[256,256]{1,0:T(8,128)}, f32[256,256]{1,0:T(8,128)}, f32[256,256]{1,0:T(8,128)}) async-done(((f32[256,256]{1,0:T(8,128)}, f32[256,256]{1,0:T(8,128)}, f32[256,256]{1,0:T(8,128)}, f32[256,256]{1,0:T(8,128)}, f32[256,256]{1,0:T(8,128)}), (f32[256,256]{1,0:T(8,128)}, f32[256,256]{1,0:T(8,128)}, f32[256,256]{1,0:T(8,128)}, ...) | async-done | bytes 1310736 | tf_op jit(solution)/shard_map/psum | solution.py:178
  600.4 71.2 %reduce-scatter.5.cloned.1.call-done = f32[8,64,512]{2,1,0:T(8,128)} async-done(((f32[8,64,2048]{2,1,0:T(8,128)}), f32[8,64,512]{2,1,0:T(8,128)}) %reduce-scatter.5.cloned.1.call-update) | async-done | bytes 1048592 | tf_op jit(solution)/shard_map/reduce_scatter | solution.py:169
  673.0 4.8 convolution_bitcast_fusion.5
  677.9 5.5 convolution_convert_fusion.2
  683.4 177.4 %reduce-scatter.3.cloned.1.call-done = f32[4,64,256]{2,1,0:T(8,128)} async-done(((f32[4,2048,256]{2,1,0:T(8,128)}), f32[4,64,256]{2,1,0:T(8,128)}) %reduce-scatter.3.cloned.1.call-update) | async-done | bytes 262160 | tf_op jit(solution)/shard_map/reduce_scatter | solution.py:137
  862.4 79.5 %all-reduce = (f32[256]{0:T(256)S(1)}, f32[128,8]{0,1:T(8,128)S(1)}) all-reduce(f32[256]{0:T(256)S(1)} %get-tuple-element.155, f32[128,8]{0,1:T(8,128)S(1)} %convolution_bitcast_fusion.5), channel_id=1, replica_groups=mesh['seq'=4,'res'=32] {'res'}, use_global_device_ids=true, to_apply=%region_12.13 | all-reduce | flops 1280 | bytes 10240 | tf_op jit(solution)/shard_map/psum | solution.py:178
  941.8 41.3 %all-reduce.2 = (f32[256]{0:T(256)}, f32[128,8]{0,1:T(8,128)}) all-reduce(f32[256]{0:T(256)S(1)} %get-tuple-element.183, f32[128,8]{0,1:T(8,128)S(1)} %get-tuple-element.184), channel_id=1, replica_groups=mesh['seq'=4,'res'=32] {'seq'}, use_global_device_ids=true, to_apply=%region_13.14 | all-reduce | flops 1280 | bytes 10240 | tf_op jit(solution)/shard_map/psum | solution.py:181
  (213 shorter events, 83.3 us)
Async XLA Ops:
  7.2 130.2 %copy-start = (bf16[256,256]{1,0:T(8,128)(2,1)S(1)}, bf16[256,256]{1,0:T(8,128)(2,1)}, u32[]{:S(2)}) copy-start(bf16[256,256]{1,0:T(8,128)(2,1)} %param.17) | copy-start | bytes 393220
  7.2 6.9 copy-start.8
  7.2 7.2 copy-start.28
  7.2 8.2 copy-start.17
  7.2 9.3 copy-start.22
  7.2 10.4 %copy-start.16 = (bf16[4,64,256]{2,1,0:T(8,128)(2,1)S(1)}, bf16[4,64,256]{2,1,0:T(8,128)(2,1)}, u32[]{:S(2)}) copy-start(bf16[4,64,256]{2,1,0:T(8,128)(2,1)} %param.14) | copy-start | bytes 393220
  7.3 10.4 %copy-start.21 = (bf16[256,256]{1,0:T(8,128)(2,1)S(1)}, bf16[256,256]{1,0:T(8,128)(2,1)}, u32[]{:S(2)}) copy-start(bf16[256,256]{1,0:T(8,128)(2,1)} %param.20) | copy-start | bytes 393220
  7.3 39.7 %all-gather.5.cloned.1.call-start = ((), (), s32[]{:S(2)}) async-start(), calls=%async_computation.3 | async-start | bytes 2621440 | tf_op jit(solution)/shard_map/all_gather | solution.py:102
  14.0 117.8 %copy-start.14 = (bf16[256,256]{1,0:T(8,128)(2,1)S(1)}, bf16[256,256]{1,0:T(8,128)(2,1)}, u32[]{:S(2)}) copy-start(bf16[256,256]{1,0:T(8,128)(2,1)} %param.18) | copy-start | bytes 393220
  14.0 117.8 %all-gather.3.cloned.1.call-start = ((), (), s32[]{:S(2)}) async-start(), calls=%async_computation.2 | async-start | bytes 4325376 | tf_op jit(solution)/shard_map/all_gather | solution.py:103
  15.2 585.2 %all-reduce.7.cloned.1.call-start = ((), (), s32[]{:S(2)}) async-start(), calls=%async_computation.6 | async-start | bytes 2621440 | tf_op jit(solution)/shard_map/psum | solution.py:178
  131.8 5.5 copy-start.4
  150.2 4.7 copy-start.1
  162.2 4.6 copy-start.3
  176.6 4.7 copy-start.1
  202.9 4.7 copy-start.1
  214.9 4.6 copy-start.3
  229.3 4.7 copy-start.1
  241.3 4.6 copy-start.3
  252.0 10.9 %copy-start.5 = (bf16[4,2048,256]{2,1,0:T(8,128)(2,1)S(1)}, bf16[4,2048,256]{2,1,0:T(8,128)(2,1)}, u32[]{:S(2)}) copy-start(bf16[4,2048,256]{2,1,0:T(8,128)(2,1)} %all-gather.3.cloned.1.call-done) | copy-start | bytes 12582916
  252.0 10.9 %copy-start.7 = (f32[4,2048,256]{1,2,0:T(8,128)S(1)}, f32[4,2048,256]{1,2,0:T(8,128)}, u32[]{:S(2)}) copy-start(f32[4,2048,256]{1,2,0:T(8,128)} %get-tuple-element.83) | copy-start | bytes 25165828
  269.1 402.6 %reduce-scatter.5.cloned.1.call-start = ((), (), s32[]{:S(2)}) async-start(), calls=%async_computation.5 | async-start | bytes 5242880 | tf_op jit(solution)/shard_map/reduce_scatter | solution.py:169
  269.7 591.1 %reduce-scatter.3.cloned.1.call-start = ((), (), s32[]{:S(2)}) async-start(), calls=%async_computation.4 | async-start | bytes 8650752 | tf_op jit(solution)/shard_map/reduce_scatter | solution.py:137
  287.3 6.7 copy-start.6
  287.3 6.7 copy-start.15
  300.5 683.5 %all-reduce.9.cloned.1.call-start = ((), (), s32[]{:S(2)}) async-start(), calls=%async_computation.7 | async-start | bytes 2621440 | tf_op jit(solution)/shard_map/psum | solution.py:181
  673.0 4.8 copy-start.30
  677.8 183.0 %copy-start.23 = (bf16[256,256]{1,0:T(8,128)(2,1)S(1)}, bf16[256,256]{1,0:T(8,128)(2,1)}, u32[]{:S(2)}) copy-start(bf16[256,256]{1,0:T(8,128)(2,1)} %param.19) | copy-start | bytes 393220
  677.8 183.0 %copy-start.29 = (f32[256]{0:T(256)S(1)}, f32[256]{0:T(256)}, u32[]{:S(2)}) copy-start(f32[256]{0:T(256)} %param.15) | copy-start | bytes 3076
  677.8 184.3 %copy-start.9 = (bf16[4,64,256]{2,1,0:T(8,128)(2,1)S(1)}, bf16[4,64,256]{2,1,0:T(8,128)(2,1)}, u32[]{:S(2)}) copy-start(bf16[4,64,256]{2,1,0:T(8,128)(2,1)} %param.12) | copy-start | bytes 393220
  677.8 184.3 %copy-start.25 = (f32[4,64]{1,0:T(4,128)S(1)}, f32[4,64]{1,0:T(4,128)}, u32[]{:S(2)}) copy-start(f32[4,64]{1,0:T(4,128)} %copy-done.24) | copy-start | bytes 3076
  677.8 184.3 %copy-start.27 = (f32[4,64]{1,0:T(4,128)S(1)}, f32[4,64]{1,0:T(4,128)}, u32[]{:S(2)}) copy-start(f32[4,64]{1,0:T(4,128)} %copy-done.26) | copy-start | bytes 3076
  (26 other events, 47.0 us)
Sparse Core Ops, SparseCore 0:
  14.1 32.7 all-gather.4
  50.6 81.1 all-gather.2
  269.2 331.1 all-reduce.6
  602.7 68.9 reduce-scatter.4
  673.9 186.8 reduce-scatter.2
  863.5 65.2 all-reduce.8
